TPU v7x, 128 devices: a whole 4x4x4 slice. The times are simulated.
128 devices in a mesh: smp: 8 (over x_lo, z), bld: 16 (over y, x_hi, core).
Axes of the slice: x: 4 (x_hi: 2, x_lo: 2; x = x_hi * 2 + x_lo), y: 4, z: 4, core: 2. Of those that a mesh axis runs over, the one named last changes fastest.
Arguments:
- tensor: bfloat16 [4, 8192, 16384], P(None, 'smp', 'bld'), may hold values from -576 to 576
- building_factor: float32 [64, 16384], P(None, 'bld'), may hold values from -144 to 144
- hour_weights: float32 [4, 64], replicated, may hold values from -5 to 5
Outputs:
- sample_factor: float32 [64, 8192], P(None, ('smp', 'bld'))
- building_out: float32 [64, 16384], P(None, ('bld', 'smp'))
- hour_out: float32 [4, 64], replicated
All inputs are finite; a program needn't handle non-finite values.
Results may differ from a plain program's by a relative error of at most 0.008.
Values may be sent and summed in bfloat16 or wider, within the bound.
A program may use at most 64 MiB of HBM per device.

v0:
```python
import math
import jax
import jax.numpy as jnp
from jax import lax
from jax.sharding import PartitionSpec as P

SWEEPS = 5
EPSILON = 1e-06
RIDGE_SHARE = 0.05


def regularized(gram):
    order_size = gram.shape[0]
    return gram + RIDGE_SHARE * jnp.mean(jnp.diagonal(gram)) * jnp.eye(order_size, dtype=gram.dtype)


def solve_rows(gram, right_side):
    lower_factor = jnp.linalg.cholesky(regularized(gram))
    middle = lax.linalg.triangular_solve(lower_factor, right_side, left_side=True, lower=True)
    return lax.linalg.triangular_solve(
        lower_factor, middle, left_side=True, lower=True, transpose_a=True
    )


def finish(unscaled, gram_raw, row_count):
    column_norm = jnp.sqrt(jnp.diagonal(gram_raw) / row_count + EPSILON)
    return (
        unscaled / column_norm[:, None],
        gram_raw / (column_norm[:, None] * column_norm[None, :]),
    )


def hour_gram(hourly):
    return jnp.dot(hourly.T, hourly, precision=lax.Precision.HIGHEST)


def self_gram(unscaled):
    return jnp.dot(unscaled, unscaled.T, precision=lax.Precision.HIGHEST)


def local(tensor, building_factor, hour_weights):
    samples_total = tensor.shape[1] * lax.axis_size("smp")
    buildings_total = tensor.shape[2] * lax.axis_size("bld")
    scale_up = math.sqrt(samples_total * buildings_total)
    hourly = hour_weights / scale_up
    gram_build = lax.psum(self_gram(building_factor), "bld")
    build_low = building_factor.astype(jnp.bfloat16)
    partial_value = jnp.einsum("rj,kij->kri", build_low, tensor, preferred_element_type=jnp.float32)
    sample_out = None
    building_out = None
    for sweep_index in range(SWEEPS):
        sample_terms = jnp.sum(hourly[:, :, None] * partial_value, axis=0)
        sample_rhs = lax.psum(sample_terms, "bld")
        unscaled = solve_rows(gram_build * hour_gram(hourly), sample_rhs)
        gram_raw = lax.psum(self_gram(unscaled), "smp")
        samples_now, gram_sample = finish(unscaled, gram_raw, samples_total)
        sample_low = samples_now.astype(jnp.bfloat16)
        share_width = samples_now.shape[1] // lax.axis_size("bld")
        sample_out = lax.dynamic_slice_in_dim(
            samples_now, lax.axis_index("bld") * share_width, share_width, 1
        )
        mixed = jnp.einsum("ri,kij->krj", sample_low, tensor, preferred_element_type=jnp.float32)
        build_terms = jnp.sum(hourly[:, :, None] * mixed, axis=0)
        build_rhs = lax.psum(build_terms, "smp")
        unscaled = solve_rows(gram_sample * hour_gram(hourly), build_rhs)
        gram_raw = lax.psum(self_gram(unscaled), "bld")
        building_now, gram_build = finish(unscaled, gram_raw, buildings_total)
        build_low = building_now.astype(jnp.bfloat16)
        share_width = building_now.shape[1] // lax.axis_size("smp")
        building_out = lax.dynamic_slice_in_dim(
            building_now, lax.axis_index("smp") * share_width, share_width, 1
        )
        partial_value = jnp.einsum(
            "rj,kij->kri", build_low, tensor, preferred_element_type=jnp.float32
        )
        hour_terms = jnp.sum(sample_low.astype(jnp.float32)[None, :, :] * partial_value, axis=2)
        hour_rhs = lax.psum(hour_terms, ("smp", "bld"))
        hourly = solve_rows(gram_sample * gram_build, hour_rhs.T).T
    return (sample_out, building_out, hourly * scale_up)


def solution(mesh):
    in_specs = (P(None, "smp", "bld"), P(None, "bld"), P())
    out_specs = (P(None, ("smp", "bld")), P(None, ("bld", "smp")), P())
    return jax.shard_map(local, mesh=mesh, in_specs=in_specs, out_specs=out_specs, check_vma=False)
```

profile of v0, /device:TPU:1, one launch (start us, length us, event | category | flops | bytes accessed | tf_op | source)
XLA Modules:
  0.0 2094.5 jit_solution(17855161390660669668)
XLA Ops:
  15.2 65.3 %psum.182 = f32[64,64]{0,1:T(8,128)S(1)} all-reduce(f32[64,64]{0,1:T(8,128)S(1)} %fusion.159), channel_id=1, replica_groups=mesh['smp'=8,'bld'=16] {'bld'}, use_global_device_ids=true, to_apply=%region_0.0 | all-reduce | flops 4096 | bytes 32768 | tf_op jit(solution)/shard_map/psum | solution.py:46
  95.0 60.6 %all-reduce.11.cloned.1.call-done = f32[64,1024]{1,0:T(8,128)} async-done(((f32[64,1024]{1,0:T(8,128)}), f32[64,1024]{1,0:T(8,128)}) %all-reduce.11.cloned.1.call-update) | async-done | bytes 262160 | tf_op jit(solution)/shard_map/psum | solution.py:53
  157.7 26.2 %psum.184 = f32[64,64]{0,1:T(8,128)S(1)} all-reduce(f32[64,64]{0,1:T(8,128)S(1)} %fusion.160), channel_id=1, replica_groups=mesh['smp'=8,'bld'=16] {'smp'}, use_global_device_ids=true, to_apply=%region_6.10 | all-reduce | flops 4096 | bytes 32768 | tf_op jit(solution)/shard_map/psum | solution.py:55
  205.1 65.8 %all-reduce.13.cloned.1.call-done = f32[64,1024]{1,0:T(8,128)} async-done(((f32[64,1024]{1,0:T(8,128)}), f32[64,1024]{1,0:T(8,128)}) %all-reduce.13.cloned.1.call-update) | async-done | bytes 262160 | tf_op jit(solution)/shard_map/psum | solution.py:64
  273.0 65.3 %psum.186 = f32[64,64]{0,1:T(8,128)S(1)} all-reduce(f32[64,64]{0,1:T(8,128)S(1)} %fusion.161), channel_id=1, replica_groups=mesh['smp'=8,'bld'=16] {'bld'}, use_global_device_ids=true, to_apply=%region_10.14 | all-reduce | flops 4096 | bytes 32768 | tf_op jit(solution)/shard_map/psum | solution.py:66
  359.6 67.3 %psum.187 = f32[64,4]{0,1:T(4,128)S(1)} all-reduce(f32[64,4]{0,1:T(4,128)S(1)} %bitcast.367), channel_id=1, replica_groups=mesh['smp'=8,'bld'=16] {'smp','bld'}, use_global_device_ids=true, to_apply=%region_13.17 | all-reduce | flops 256 | bytes 2048 | tf_op jit(solution)/shard_map/psum | solution.py:77
  442.7 127.8 %all-reduce.15.cloned.1.call-done = f32[64,1024]{1,0:T(8,128)} async-done(((f32[64,1024]{1,0:T(8,128)}), f32[64,1024]{1,0:T(8,128)}) %all-reduce.15.cloned.1.call-update) | async-done | bytes 262160 | tf_op jit(solution)/shard_map/psum | solution.py:53
  572.6 26.5 %psum.189 = f32[64,64]{0,1:T(8,128)S(1)} all-reduce(f32[64,64]{0,1:T(8,128)S(1)} %fusion.162), channel_id=1, replica_groups=mesh['smp'=8,'bld'=16] {'smp'}, use_global_device_ids=true, to_apply=%region_17.23 | all-reduce | flops 4096 | bytes 32768 | tf_op jit(solution)/shard_map/psum | solution.py:55
  620.2 65.8 %all-reduce.17.cloned.1.call-done = f32[64,1024]{1,0:T(8,128)} async-done(((f32[64,1024]{1,0:T(8,128)}), f32[64,1024]{1,0:T(8,128)}) %all-reduce.17.cloned.1.call-update) | async-done | bytes 262160 | tf_op jit(solution)/shard_map/psum | solution.py:64
  688.1 64.7 %psum.191 = f32[64,64]{0,1:T(8,128)S(1)} all-reduce(f32[64,64]{0,1:T(8,128)S(1)} %fusion.163), channel_id=1, replica_groups=mesh['smp'=8,'bld'=16] {'bld'}, use_global_device_ids=true, to_apply=%region_21.27 | all-reduce | flops 4096 | bytes 32768 | tf_op jit(solution)/shard_map/psum | solution.py:66
  774.2 67.5 %psum.192 = f32[64,4]{0,1:T(4,128)S(1)} all-reduce(f32[64,4]{0,1:T(4,128)S(1)} %bitcast.368), channel_id=1, replica_groups=mesh['smp'=8,'bld'=16] {'smp','bld'}, use_global_device_ids=true, to_apply=%region_24.30 | all-reduce | flops 256 | bytes 2048 | tf_op jit(solution)/shard_map/psum | solution.py:77
  857.5 127.8 %all-reduce.19.cloned.1.call-done = f32[64,1024]{1,0:T(8,128)} async-done(((f32[64,1024]{1,0:T(8,128)}), f32[64,1024]{1,0:T(8,128)}) %all-reduce.19.cloned.1.call-update) | async-done | bytes 262160 | tf_op jit(solution)/shard_map/psum | solution.py:53
  1034.7 65.8 %all-reduce.21.cloned.1.call-done = f32[64,1024]{1,0:T(8,128)} async-done(((f32[64,1024]{1,0:T(8,128)}), f32[64,1024]{1,0:T(8,128)}) %all-reduce.21.cloned.1.call-update) | async-done | bytes 262160 | tf_op jit(solution)/shard_map/psum | solution.py:64
  1102.6 65.2 %psum.196 = f32[64,64]{0,1:T(8,128)S(1)} all-reduce(f32[64,64]{0,1:T(8,128)S(1)} %fusion.165), channel_id=1, replica_groups=mesh['smp'=8,'bld'=16] {'bld'}, use_global_device_ids=true, to_apply=%region_32.38 | all-reduce | flops 4096 | bytes 32768 | tf_op jit(solution)/shard_map/psum | solution.py:66
  1189.1 67.3 %psum.197 = f32[64,4]{0,1:T(4,128)S(1)} all-reduce(f32[64,4]{0,1:T(4,128)S(1)} %bitcast.369), channel_id=1, replica_groups=mesh['smp'=8,'bld'=16] {'smp','bld'}, use_global_device_ids=true, to_apply=%region_35.41 | all-reduce | flops 256 | bytes 2048 | tf_op jit(solution)/shard_map/psum | solution.py:77
  1272.2 127.8 %all-reduce.23.cloned.1.call-done = f32[64,1024]{1,0:T(8,128)} async-done(((f32[64,1024]{1,0:T(8,128)}), f32[64,1024]{1,0:T(8,128)}) %all-reduce.23.cloned.1.call-update) | async-done | bytes 262160 | tf_op jit(solution)/shard_map/psum | solution.py:53
  1402.0 26.5 %psum.199 = f32[64,64]{0,1:T(8,128)S(1)} all-reduce(f32[64,64]{0,1:T(8,128)S(1)} %fusion.166), channel_id=1, replica_groups=mesh['smp'=8,'bld'=16] {'smp'}, use_global_device_ids=true, to_apply=%region_39.45 | all-reduce | flops 4096 | bytes 32768 | tf_op jit(solution)/shard_map/psum | solution.py:55
  1449.7 65.8 %all-reduce.25.cloned.1.call-done = f32[64,1024]{1,0:T(8,128)} async-done(((f32[64,1024]{1,0:T(8,128)}), f32[64,1024]{1,0:T(8,128)}) %all-reduce.25.cloned.1.call-update) | async-done | bytes 262160 | tf_op jit(solution)/shard_map/psum | solution.py:64
  1517.6 64.7 %psum.201 = f32[64,64]{0,1:T(8,128)S(1)} all-reduce(f32[64,64]{0,1:T(8,128)S(1)} %fusion.167), channel_id=1, replica_groups=mesh['smp'=8,'bld'=16] {'bld'}, use_global_device_ids=true, to_apply=%region_43.49 | all-reduce | flops 4096 | bytes 32768 | tf_op jit(solution)/shard_map/psum | solution.py:66
  1603.6 67.5 %psum.202 = f32[64,4]{0,1:T(4,128)S(1)} all-reduce(f32[64,4]{0,1:T(4,128)S(1)} %bitcast.370), channel_id=1, replica_groups=mesh['smp'=8,'bld'=16] {'smp','bld'}, use_global_device_ids=true, to_apply=%region_46.52 | all-reduce | flops 256 | bytes 2048 | tf_op jit(solution)/shard_map/psum | solution.py:77
  1686.9 127.8 %all-reduce.27.cloned.1.call-done = f32[64,1024]{1,0:T(8,128)} async-done(((f32[64,1024]{1,0:T(8,128)}), f32[64,1024]{1,0:T(8,128)}) %all-reduce.27.cloned.1.call-update) | async-done | bytes 262160 | tf_op jit(solution)/shard_map/psum | solution.py:53
  1864.7 65.3 %all-reduce.29.cloned.1.call-done = f32[64,1024]{1,0:T(8,128)} async-done(((f32[64,1024]{1,0:T(8,128)}), f32[64,1024]{1,0:T(8,128)}) %all-reduce.29.cloned.1.call-update) | async-done | bytes 262160 | tf_op jit(solution)/shard_map/psum | solution.py:64
  1932.1 65.0 %psum.206 = f32[64,64]{0,1:T(8,128)S(1)} all-reduce(f32[64,64]{0,1:T(8,128)S(1)} %fusion.169), channel_id=1, replica_groups=mesh['smp'=8,'bld'=16] {'bld'}, use_global_device_ids=true, to_apply=%region_54.60 | all-reduce | flops 4096 | bytes 32768 | tf_op jit(solution)/shard_map/psum | solution.py:66
  2018.5 67.3 %psum.207 = f32[64,4]{0,1:T(4,128)S(1)} all-reduce(f32[64,4]{0,1:T(4,128)S(1)} %fusion.11), channel_id=1, replica_groups=mesh['smp'=8,'bld'=16] {'smp','bld'}, use_global_device_ids=true, to_apply=%region_57.63 | all-reduce | flops 256 | bytes 2048 | tf_op jit(solution)/shard_map/psum | solution.py:77
  (277 shorter events, 362.7 us)
Async XLA Ops:
  7.2 73.3 %copy-start.1 = (f32[4,64]{1,0:T(4,128)S(1)}, f32[4,64]{1,0:T(4,128)}, u32[]{:S(2)}) copy-start(f32[4,64]{1,0:T(4,128)} %param.14) | copy-start | bytes 3076
  7.2 7.6 copy-start
  7.2 148.4 %all-reduce.11.cloned.1.call-start = ((), (), s32[]{:S(2)}) async-start(), calls=%async_computation | async-start | bytes 524288 | tf_op jit(solution)/shard_map/psum | solution.py:53
  14.7 256.2 %all-reduce.13.cloned.1.call-start = ((), (), s32[]{:S(2)}) async-start(), calls=%async_computation.1 | async-start | bytes 524288 | tf_op jit(solution)/shard_map/psum | solution.py:64
  199.4 371.1 %all-reduce.15.cloned.1.call-start = ((), (), s32[]{:S(2)}) async-start(), calls=%async_computation.2 | async-start | bytes 524288 | tf_op jit(solution)/shard_map/psum | solution.py:53
  436.5 249.5 %all-reduce.17.cloned.1.call-start = ((), (), s32[]{:S(2)}) async-start(), calls=%async_computation.3 | async-start | bytes 524288 | tf_op jit(solution)/shard_map/psum | solution.py:64
  614.5 370.8 %all-reduce.19.cloned.1.call-start = ((), (), s32[]{:S(2)}) async-start(), calls=%async_computation.4 | async-start | bytes 524288 | tf_op jit(solution)/shard_map/psum | solution.py:53
  851.2 249.2 %all-reduce.21.cloned.1.call-start = ((), (), s32[]{:S(2)}) async-start(), calls=%async_computation.5 | async-start | bytes 524288 | tf_op jit(solution)/shard_map/psum | solution.py:64
  1029.0 371.0 %all-reduce.23.cloned.1.call-start = ((), (), s32[]{:S(2)}) async-start(), calls=%async_computation.6 | async-start | bytes 524288 | tf_op jit(solution)/shard_map/psum | solution.py:53
  1265.9 249.5 %all-reduce.25.cloned.1.call-start = ((), (), s32[]{:S(2)}) async-start(), calls=%async_computation.7 | async-start | bytes 524288 | tf_op jit(solution)/shard_map/psum | solution.py:64
  1443.9 370.8 %all-reduce.27.cloned.1.call-start = ((), (), s32[]{:S(2)}) async-start(), calls=%async_computation.8 | async-start | bytes 524288 | tf_op jit(solution)/shard_map/psum | solution.py:53
  1680.7 249.3 %all-reduce.29.cloned.1.call-start = ((), (), s32[]{:S(2)}) async-start(), calls=%async_computation.9 | async-start | bytes 524288 | tf_op jit(solution)/shard_map/psum | solution.py:64
Sparse Core Ops, SparseCore 0:
  14.8 140.7 all-reduce.10
  199.5 71.3 all-reduce.12
  436.6 133.8 all-reduce.14
  614.6 71.3 all-reduce.16
  851.4 133.8 all-reduce.18
  1029.1 71.3 all-reduce.20
  1266.0 133.8 all-reduce.22
  1444.1 71.3 all-reduce.24
  1680.8 133.8 all-reduce.26
  1858.6 71.3 all-reduce.28
where the time goes:
time: 2100 us; the launch traced here: 2090 us
  waiting for transfers between devices  900 us (43%)
  blocking collectives  859 us (41%)
  other arithmetic  196 us (9%)
  matrix products  90.9 us (4%)
  between operations  25.1 us (1%)
  local copies, waits for them, and re-layouts  22.6 us (1%)
    psum x5, waiting for transfers between devices, local(): sample_rhs = lax.psum(sample_terms, 'bld')  572 us
    psum x5, blocking collectives, local(): hour_rhs = lax.psum(hour_terms, ('smp', 'bld'))  337 us
    psum x5, waiting for transfers between devices, local(): build_rhs = lax.psum(build_terms, 'smp')  328 us
    psum x5, blocking collectives, local(): gram_raw = lax.psum(self_gram(unscaled), 'bld')  325 us
    psum x5, blocking collectives, local(): gram_raw = lax.psum(self_gram(unscaled), 'smp')  132 us
    another operation x45, other arithmetic, solve_rows(): lower_factor = jnp.linalg.cholesky(regularized(gram))  97.7 us
    another operation x30, other arithmetic, solve_rows(): lax.linalg.triangular_solve(lower_factor, middle, left_side=True, lower=T...  83.3 us
    psum x1, blocking collectives, local(): gram_build = lax.psum(self_gram(building_factor), 'bld')  65.3 us
  transfers between devices with their start and end apart: 10, of which 10 were waited for; matrix products, arithmetic and copies ran while one was open for 3% of the time, Pallas kernels for 0%

commit v1 on v0

--- a/solution.py
+++ b/solution.py
@@ -7,6 +7,11 @@
 SWEEPS = 5
 EPSILON = 1e-06
 RIDGE_SHARE = 0.05
+
+
+def one_after_other(array, inner_axis, outer_axis):
+    partial = lax.psum(array, inner_axis)
+    return lax.psum(partial, outer_axis)
 
 
 def regularized(gram):
@@ -74,7 +79,7 @@
             "rj,kij->kri", build_low, tensor, preferred_element_type=jnp.float32
         )
         hour_terms = jnp.sum(sample_low.astype(jnp.float32)[None, :, :] * partial_value, axis=2)
-        hour_rhs = lax.psum(hour_terms, ("smp", "bld"))
+        hour_rhs = one_after_other(hour_terms, "smp", "bld")
         hourly = solve_rows(gram_sample * gram_build, hour_rhs.T).T
     return (sample_out, building_out, hourly * scale_up)
 

time: 2100 us -> 2030 us (0.967)
  blocking collectives: 859 us -> 801 us
    psum x5 -> x10, blocking collectives: 337 us -> 279 us  [the longest x5 211 us: one_after_other(): return lax.psum(partial, outer_axis)]
where the time goes in v1:
time: 2030 us
  waiting for transfers between devices  888 us (44%)
  blocking collectives  801 us (39%)
  other arithmetic  196 us (10%)
  matrix products  90.9 us (4%)
  between operations  25.4 us (1%)
  local copies, waits for them, and re-layouts  22.6 us (1%)
    psum x5, waiting for transfers between devices, local(): sample_rhs = lax.psum(sample_terms, 'bld')  561 us
    psum x5, waiting for transfers between devices, local(): build_rhs = lax.psum(build_terms, 'smp')  327 us
    psum x5, blocking collectives, local(): gram_raw = lax.psum(self_gram(unscaled), 'bld')  324 us
    psum x5, blocking collectives, one_after_other(): return lax.psum(partial, outer_axis)  211 us
    psum x5, blocking collectives, local(): gram_raw = lax.psum(self_gram(unscaled), 'smp')  132 us
    another operation x45, other arithmetic, solve_rows(): lower_factor = jnp.linalg.cholesky(regularized(gram))  97.7 us
    another operation x30, other arithmetic, solve_rows(): lax.linalg.triangular_solve(lower_factor, middle, left_side=True, lower=T...  83.3 us
    psum x5, blocking collectives, one_after_other(): partial = lax.psum(array, inner_axis)  68.5 us
  transfers between devices with their start and end apart: 10, of which 10 were waited for; matrix products, arithmetic and copies ran while one was open for 3% of the time, Pallas kernels for 0%

profile of v1, /device:TPU:1, one launch (start us, length us, event | category | flops | bytes accessed | tf_op | source)
XLA Modules:
  0.0 2025.4 jit_solution(12484149870965406778)
XLA Ops:
  15.2 65.3 %psum.217 = f32[64,64]{0,1:T(8,128)S(1)} all-reduce(f32[64,64]{0,1:T(8,128)S(1)} %fusion.159), channel_id=1, replica_groups=mesh['smp'=8,'bld'=16] {'bld'}, use_global_device_ids=true, to_apply=%region_0.0 | all-reduce | flops 4096 | bytes 32768 | tf_op jit(solution)/shard_map/psum | solution.py:51
  95.0 60.6 %all-reduce.11.cloned.1.call-done = f32[64,1024]{1,0:T(8,128)} async-done(((f32[64,1024]{1,0:T(8,128)}), f32[64,1024]{1,0:T(8,128)}) %all-reduce.11.cloned.1.call-update) | async-done | bytes 262160 | tf_op jit(solution)/shard_map/psum | solution.py:58
  157.7 26.2 %psum.219 = f32[64,64]{0,1:T(8,128)S(1)} all-reduce(f32[64,64]{0,1:T(8,128)S(1)} %fusion.160), channel_id=1, replica_groups=mesh['smp'=8,'bld'=16] {'smp'}, use_global_device_ids=true, to_apply=%region_6.10 | all-reduce | flops 4096 | bytes 32768 | tf_op jit(solution)/shard_map/psum | solution.py:60
  205.1 65.8 %all-reduce.13.cloned.1.call-done = f32[64,1024]{1,0:T(8,128)} async-done(((f32[64,1024]{1,0:T(8,128)}), f32[64,1024]{1,0:T(8,128)}) %all-reduce.13.cloned.1.call-update) | async-done | bytes 262160 | tf_op jit(solution)/shard_map/psum | solution.py:69
  273.0 65.0 %psum.221 = f32[64,64]{0,1:T(8,128)S(1)} all-reduce(f32[64,64]{0,1:T(8,128)S(1)} %fusion.161), channel_id=1, replica_groups=mesh['smp'=8,'bld'=16] {'bld'}, use_global_device_ids=true, to_apply=%region_10.14 | all-reduce | flops 4096 | bytes 32768 | tf_op jit(solution)/shard_map/psum | solution.py:71
  373.0 42.1 %psum.223 = f32[64,4]{0,1:T(4,128)S(1)} all-reduce(f32[64,4]{0,1:T(4,128)S(1)} %bitcast.370), channel_id=1, replica_groups=mesh['smp'=8,'bld'=16] {'bld'}, use_global_device_ids=true, to_apply=%region_14.18 | all-reduce | flops 256 | bytes 2048 | tf_op jit(solution)/shard_map/psum | solution.py:14
  430.9 125.2 %all-reduce.15.cloned.1.call-done = f32[64,1024]{1,0:T(8,128)} async-done(((f32[64,1024]{1,0:T(8,128)}), f32[64,1024]{1,0:T(8,128)}) %all-reduce.15.cloned.1.call-update) | async-done | bytes 262160 | tf_op jit(solution)/shard_map/psum | solution.py:58
  558.2 26.5 %psum.225 = f32[64,64]{0,1:T(8,128)S(1)} all-reduce(f32[64,64]{0,1:T(8,128)S(1)} %fusion.162), channel_id=1, replica_groups=mesh['smp'=8,'bld'=16] {'smp'}, use_global_device_ids=true, to_apply=%region_18.24 | all-reduce | flops 4096 | bytes 32768 | tf_op jit(solution)/shard_map/psum | solution.py:60
  606.3 65.0 %all-reduce.17.cloned.1.call-done = f32[64,1024]{1,0:T(8,128)} async-done(((f32[64,1024]{1,0:T(8,128)}), f32[64,1024]{1,0:T(8,128)}) %all-reduce.17.cloned.1.call-update) | async-done | bytes 262160 | tf_op jit(solution)/shard_map/psum | solution.py:69
  673.4 64.7 %psum.227 = f32[64,64]{0,1:T(8,128)S(1)} all-reduce(f32[64,64]{0,1:T(8,128)S(1)} %fusion.163), channel_id=1, replica_groups=mesh['smp'=8,'bld'=16] {'bld'}, use_global_device_ids=true, to_apply=%region_22.28 | all-reduce | flops 4096 | bytes 32768 | tf_op jit(solution)/shard_map/psum | solution.py:71
  773.2 42.1 %psum.229 = f32[64,4]{0,1:T(4,128)S(1)} all-reduce(f32[64,4]{0,1:T(4,128)S(1)} %bitcast.371), channel_id=1, replica_groups=mesh['smp'=8,'bld'=16] {'bld'}, use_global_device_ids=true, to_apply=%region_26.32 | all-reduce | flops 256 | bytes 2048 | tf_op jit(solution)/shard_map/psum | solution.py:14
  831.1 125.2 %all-reduce.19.cloned.1.call-done = f32[64,1024]{1,0:T(8,128)} async-done(((f32[64,1024]{1,0:T(8,128)}), f32[64,1024]{1,0:T(8,128)}) %all-reduce.19.cloned.1.call-update) | async-done | bytes 262160 | tf_op jit(solution)/shard_map/psum | solution.py:58
  958.4 26.8 %psum.231 = f32[64,64]{0,1:T(8,128)S(1)} all-reduce(f32[64,64]{0,1:T(8,128)S(1)} %fusion.164), channel_id=1, replica_groups=mesh['smp'=8,'bld'=16] {'smp'}, use_global_device_ids=true, to_apply=%region_30.36 | all-reduce | flops 4096 | bytes 32768 | tf_op jit(solution)/shard_map/psum | solution.py:60
  1006.3 65.4 %all-reduce.21.cloned.1.call-done = f32[64,1024]{1,0:T(8,128)} async-done(((f32[64,1024]{1,0:T(8,128)}), f32[64,1024]{1,0:T(8,128)}) %all-reduce.21.cloned.1.call-update) | async-done | bytes 262160 | tf_op jit(solution)/shard_map/psum | solution.py:69
  1073.8 64.7 %psum.233 = f32[64,64]{0,1:T(8,128)S(1)} all-reduce(f32[64,64]{0,1:T(8,128)S(1)} %fusion.165), channel_id=1, replica_groups=mesh['smp'=8,'bld'=16] {'bld'}, use_global_device_ids=true, to_apply=%region_34.40 | all-reduce | flops 4096 | bytes 32768 | tf_op jit(solution)/shard_map/psum | solution.py:71
  1173.6 42.1 %psum.235 = f32[64,4]{0,1:T(4,128)S(1)} all-reduce(f32[64,4]{0,1:T(4,128)S(1)} %bitcast.372), channel_id=1, replica_groups=mesh['smp'=8,'bld'=16] {'bld'}, use_global_device_ids=true, to_apply=%region_38.44 | all-reduce | flops 256 | bytes 2048 | tf_op jit(solution)/shard_map/psum | solution.py:14
  1231.7 124.7 %all-reduce.23.cloned.1.call-done = f32[64,1024]{1,0:T(8,128)} async-done(((f32[64,1024]{1,0:T(8,128)}), f32[64,1024]{1,0:T(8,128)}) %all-reduce.23.cloned.1.call-update) | async-done | bytes 262160 | tf_op jit(solution)/shard_map/psum | solution.py:58
  1405.8 65.8 %all-reduce.25.cloned.1.call-done = f32[64,1024]{1,0:T(8,128)} async-done(((f32[64,1024]{1,0:T(8,128)}), f32[64,1024]{1,0:T(8,128)}) %all-reduce.25.cloned.1.call-update) | async-done | bytes 262160 | tf_op jit(solution)/shard_map/psum | solution.py:69
  1473.7 64.7 %psum.239 = f32[64,64]{0,1:T(8,128)S(1)} all-reduce(f32[64,64]{0,1:T(8,128)S(1)} %fusion.167), channel_id=1, replica_groups=mesh['smp'=8,'bld'=16] {'bld'}, use_global_device_ids=true, to_apply=%region_46.52 | all-reduce | flops 4096 | bytes 32768 | tf_op jit(solution)/shard_map/psum | solution.py:71
  1573.5 42.4 %psum.241 = f32[64,4]{0,1:T(4,128)S(1)} all-reduce(f32[64,4]{0,1:T(4,128)S(1)} %bitcast.373), channel_id=1, replica_groups=mesh['smp'=8,'bld'=16] {'bld'}, use_global_device_ids=true, to_apply=%region_50.56 | all-reduce | flops 256 | bytes 2048 | tf_op jit(solution)/shard_map/psum | solution.py:14
  1631.6 125.2 %all-reduce.27.cloned.1.call-done = f32[64,1024]{1,0:T(8,128)} async-done(((f32[64,1024]{1,0:T(8,128)}), f32[64,1024]{1,0:T(8,128)}) %all-reduce.27.cloned.1.call-update) | async-done | bytes 262160 | tf_op jit(solution)/shard_map/psum | solution.py:58
  1806.9 65.2 %all-reduce.29.cloned.1.call-done = f32[64,1024]{1,0:T(8,128)} async-done(((f32[64,1024]{1,0:T(8,128)}), f32[64,1024]{1,0:T(8,128)}) %all-reduce.29.cloned.1.call-update) | async-done | bytes 262160 | tf_op jit(solution)/shard_map/psum | solution.py:69
  1874.2 65.0 %psum.245 = f32[64,64]{0,1:T(8,128)S(1)} all-reduce(f32[64,64]{0,1:T(8,128)S(1)} %fusion.169), channel_id=1, replica_groups=mesh['smp'=8,'bld'=16] {'bld'}, use_global_device_ids=true, to_apply=%region_58.64 | all-reduce | flops 4096 | bytes 32768 | tf_op jit(solution)/shard_map/psum | solution.py:71
  1974.4 42.1 %psum.247 = f32[64,4]{0,1:T(4,128)S(1)} all-reduce(f32[64,4]{0,1:T(4,128)S(1)} %bitcast.374), channel_id=1, replica_groups=mesh['smp'=8,'bld'=16] {'bld'}, use_global_device_ids=true, to_apply=%region_62.68 | all-reduce | flops 256 | bytes 2048 | tf_op jit(solution)/shard_map/psum | solution.py:14
  (282 shorter events, 431.9 us)
Async XLA Ops:
  7.2 73.3 %copy-start.1 = (f32[4,64]{1,0:T(4,128)S(1)}, f32[4,64]{1,0:T(4,128)}, u32[]{:S(2)}) copy-start(f32[4,64]{1,0:T(4,128)} %param.14) | copy-start | bytes 3076
  7.2 7.6 copy-start
  7.2 148.4 %all-reduce.11.cloned.1.call-start = ((), (), s32[]{:S(2)}) async-start(), calls=%async_computation | async-start | bytes 524288 | tf_op jit(solution)/shard_map/psum | solution.py:58
  14.7 256.2 %all-reduce.13.cloned.1.call-start = ((), (), s32[]{:S(2)}) async-start(), calls=%async_computation.1 | async-start | bytes 524288 | tf_op jit(solution)/shard_map/psum | solution.py:69
  199.4 356.7 %all-reduce.15.cloned.1.call-start = ((), (), s32[]{:S(2)}) async-start(), calls=%async_computation.2 | async-start | bytes 524288 | tf_op jit(solution)/shard_map/psum | solution.py:58
  424.7 246.6 %all-reduce.17.cloned.1.call-start = ((), (), s32[]{:S(2)}) async-start(), calls=%async_computation.3 | async-start | bytes 524288 | tf_op jit(solution)/shard_map/psum | solution.py:69
  600.1 356.1 %all-reduce.19.cloned.1.call-start = ((), (), s32[]{:S(2)}) async-start(), calls=%async_computation.4 | async-start | bytes 524288 | tf_op jit(solution)/shard_map/psum | solution.py:58
  824.8 246.9 %all-reduce.21.cloned.1.call-start = ((), (), s32[]{:S(2)}) async-start(), calls=%async_computation.5 | async-start | bytes 524288 | tf_op jit(solution)/shard_map/psum | solution.py:69
  1000.6 355.8 %all-reduce.23.cloned.1.call-start = ((), (), s32[]{:S(2)}) async-start(), calls=%async_computation.6 | async-start | bytes 524288 | tf_op jit(solution)/shard_map/psum | solution.py:58
  1225.3 246.4 %all-reduce.25.cloned.1.call-start = ((), (), s32[]{:S(2)}) async-start(), calls=%async_computation.7 | async-start | bytes 524288 | tf_op jit(solution)/shard_map/psum | solution.py:69
  1400.1 356.7 %all-reduce.27.cloned.1.call-start = ((), (), s32[]{:S(2)}) async-start(), calls=%async_computation.8 | async-start | bytes 524288 | tf_op jit(solution)/shard_map/psum | solution.py:58
  1625.4 246.7 %all-reduce.29.cloned.1.call-start = ((), (), s32[]{:S(2)}) async-start(), calls=%async_computation.9 | async-start | bytes 524288 | tf_op jit(solution)/shard_map/psum | solution.py:69
Sparse Core Ops, SparseCore 0:
  14.8 140.7 all-reduce.10
  199.5 71.3 all-reduce.12
  424.8 131.2 all-reduce.14
  600.2 70.9 all-reduce.16
  825.0 131.2 all-reduce.18
  1000.7 70.9 all-reduce.20
  1225.4 130.9 all-reduce.22
  1400.2 71.3 all-reduce.24
  1625.5 131.2 all-reduce.26
  1800.7 71.3 all-reduce.28
